TPU v7x, 256 devices: a whole 4x4x8 slice. The times are simulated.
256 devices in a mesh: leaf: 2 (over core), row: 4 (over x), col: 32 (over z, y).
Axes of the slice: x: 4, y: 4, z: 8, core: 2. Of those that a mesh axis runs over, the one named last changes fastest.
Arguments:
- child_rhs: float32 [512, 256, 256], P(('leaf', 'row', 'col')), may hold values from -6 to 6
- child_diag: float32 [512, 256, 256], P(('leaf', 'row', 'col')), may hold values from -0.375 to 0.375
- child_off: float32 [512, 256, 256], P(('leaf', 'row', 'col')), may hold values from -0.046875 to 0.046875
- live: int32 [512], P(('leaf', 'row', 'col')), may hold values from 1 to 256, 81920 in all
- targets: int32 [512, 256], P(('leaf', 'row', 'col')), may hold values from 0 to 2047
- top_rhs: float32 [2048, 256], P('row'), may hold values from -6 to 6
- top_factor: float32 [2048, 2048], P('row', 'col'), may hold values from -0.125 to 0.125
- top_diag: float32 [2048, 512], P('row'), may hold values from -0.25 to 0.25
Outputs:
- child_sol: float32 [512, 256, 256], P(('leaf', 'row', 'col'))
- top_sol: float32 [2048, 256], P('row')
All inputs are finite; a program needn't handle non-finite values. No bound on the sum of `live` on one device may be relied on, other than what follows from the above.
Results may differ from a plain program's by a relative error of at most 0.0003.
Values sent between devices are 32-bit elements; how exact they have to be, the bound alone decides.
A program may use at most 64 MiB of HBM per device.

v0:
```python
import jax
import jax.numpy as jnp
from jax import lax
from jax.sharding import PartitionSpec as P


def spread(value, axis, source):
    kept = jnp.where(lax.axis_index(axis) == source, value, 0).astype(value.dtype)
    return lax.psum(kept, axis)


def unit_lower(matrix):
    return jnp.tril(matrix) + jnp.eye(matrix.shape[-1], dtype=matrix.dtype)


def shards(child_rhs, child_diag, child_off, live, targets, top_rhs, top_factor, top_diag):
    highest = lax.Precision.HIGHEST
    owned_rows = top_rhs.shape[0]
    right_count = top_rhs.shape[1]
    block_size = top_diag.shape[1]
    owned_blocks = owned_rows // block_size
    row_count = lax.axis_size("row")
    top_order = owned_rows * row_count
    col_width = top_factor.shape[1]
    my_row = lax.axis_index("row")
    my_col = lax.axis_index("col")
    child_sol = jnp.einsum("bij,bjr->bir", unit_lower(child_diag), child_rhs, precision=highest)
    tiles = jnp.einsum("btj,bjr->btr", child_off, child_sol, precision=highest)
    slot_index = jnp.arange(child_off.shape[1], dtype=jnp.int32)
    keep = slot_index[None, :] < live[:, None]
    tiles = jnp.where(keep[:, :, None], tiles, jnp.zeros_like(tiles))
    contrib = jnp.zeros((top_order, right_count), jnp.float32)
    contrib = contrib.at[targets.reshape(-1)].add(tiles.reshape(-1, right_count))
    row_part = lax.psum_scatter(contrib, "row", scatter_dimension=0, tiled=True)
    share = lax.psum_scatter(row_part, ("leaf", "col"), scatter_dimension=0, tiled=True)
    updates = lax.all_gather(share, ("leaf", "col"), axis=0, tiled=True)
    reduced = top_rhs - updates
    inverse_all = unit_lower(top_diag.reshape(owned_blocks, block_size, block_size))
    col_global = my_col * col_width + jnp.arange(col_width, dtype=jnp.int32)

    def step(block, solution):
        local = block % owned_blocks
        owner = block // owned_blocks
        factor_rows = top_factor
        factor_rows = jnp.where(
            (col_global < block * block_size)[None, :], factor_rows, jnp.zeros_like(factor_rows)
        )
        columns = lax.dynamic_slice_in_dim(solution, my_col * col_width, col_width, 0)
        partial_value = jnp.dot(
            factor_rows, columns, precision=highest, preferred_element_type=jnp.float32
        )
        block_inverse = lax.dynamic_index_in_dim(inverse_all, local, 0, keepdims=False)
        before = lax.psum(partial_value, "col")
        solved = jnp.dot(
            block_inverse, reduced - before, precision=highest, preferred_element_type=jnp.float32
        )
        solved = spread(solved, "row", owner)
        return lax.dynamic_update_slice_in_dim(solution, solved, block * block_size, 0)

    solution = lax.fori_loop(
        0, row_count * owned_blocks, step, jnp.zeros((top_order, right_count), jnp.float32)
    )
    top_sol = lax.dynamic_slice_in_dim(solution, my_row * owned_rows, owned_rows, 0)
    return (child_sol, top_sol)


def solution(mesh):
    in_specs = (
        P(("leaf", "row", "col"), None, None),
        P(("leaf", "row", "col"), None, None),
        P(("leaf", "row", "col"), None, None),
        P(("leaf", "row", "col")),
        P(("leaf", "row", "col"), None),
        P("row", None),
        P("row", "col"),
        P("row", None),
    )
    out_specs = (P(("leaf", "row", "col"), None, None), P("row", None))
    return jax.shard_map(shards, mesh=mesh, in_specs=in_specs, out_specs=out_specs, check_vma=False)
```

profile of v0, /device:TPU:8, one launch (start us, length us, event | category | flops | bytes accessed | tf_op | source)
XLA Modules:
  0.0 1160.2 jit_solution(9631845340324377303)
XLA Ops:
  7.2 0.0 reduce-scatter.3.cloned.1.call-start
  7.3 0.8 iota_compare_fusion.4
  8.1 0.7 copy.18
  8.8 1.2 copy.10
  10.0 1.1 fusion.14
  11.1 0.7 convolution_select_fusion.1
  11.8 4.7 scatter_custom_fusion
  16.5 0.0 reduce-scatter.3.cloned.1.call-update
  16.6 0.0 reduce-scatter.5.cloned.1.call-start
  16.6 35.2 %reduce-scatter.3.cloned.1.call-done = f32[512,256]{1,0:T(8,128)} async-done(((f32[2048,256]{1,0:T(8,128)}), f32[512,256]{1,0:T(8,128)}) %reduce-scatter.3.cloned.1.call-update) | async-done | bytes 524304 | tf_op jit(solution)/shard_map/reduce_scatter | solution.py:34
  51.8 0.1 add_bitcast_fusion
  52.0 142.3 %reduce-scatter.5.cloned.1.call-done = f32[8,256]{1,0:T(8,128)} async-done(((f32[512,256]{1,0:T(8,128)}), f32[8,256]{1,0:T(8,128)}) %reduce-scatter.5.cloned.1.call-update) | async-done | bytes 8208 | tf_op jit(solution)/shard_map/reduce_scatter | solution.py:35
  194.3 126.2 %all_gather.3 = f32[512,256]{1,0:T(8,128)S(1)} all-gather(f32[8,256]{1,0:T(8,128)} %reduce-scatter.5.cloned.1.call-done), channel_id=1, replica_groups=mesh['leaf'=2,'row'=4,'col'=32] {'leaf','col'}, dimensions={0}, use_global_device_ids=true | all-gather | bytes 532480 | tf_op jit(solution)/shard_map/all_gather | solution.py:36
  320.5 0.1 sub.17
  320.6 1.5 broadcast.60.clone
  322.0 829.5 %while.16 = (s32[]{:T(128)}, f32[2048,256]{1,0:T(8,128)}, f32[512,64]{0,1:T(8,128)S(1)}, s32[]{:T(128)}, f32[512,256]{1,0:T(8,128)S(1)}, /*index=5*/f32[1,512,51...) while((s32[]{:T(128)}, f32[2048,256]{1,0:T(8,128)}, ...), condition=%wide.region_6.7_spmd.clone, body=%wide.region_3.6_spmd.clone.sunk | while | flops 906526848 | bytes 11731889 | solution.py:60
  322.1 2.3 fusion.35
  324.4 0.0 all-reduce.5.cloned.1.call-start
  324.5 162.3 %all-reduce.3.cloned.1.call-done = f32[512,256]{1,0:T(8,128)} async-done(((f32[512,256]{1,0:T(8,128)}), f32[512,256]{1,0:T(8,128)}) %all-reduce.3.cloned.1.call-update) | async-done | bytes 524304 | tf_op jit(solution)/shard_map/while/body/eval_jaxpr/psum | solution.py:53
  486.8 3.7 fusion.36
  490.5 46.3 %all-reduce.5.cloned.1.call-done = f32[512,256]{0,1:T(8,128)} async-done(((f32[512,256]{0,1:T(8,128)}), f32[512,256]{0,1:T(8,128)}) %all-reduce.5.cloned.1.call-update) | async-done | bytes 524304 | tf_op jit(solution)/shard_map/while/body/eval_jaxpr/psum | solution.py:9
  536.8 1.2 copy.20
  538.0 0.8 constant_dynamic-update-slice_fusion.2
  538.9 2.3 fusion.35
  541.2 0.0 all-reduce.3.cloned.1.call-update
  541.2 0.0 all-reduce.5.cloned.1.call-start
  541.3 149.5 %all-reduce.3.cloned.1.call-done = f32[512,256]{1,0:T(8,128)} async-done(((f32[512,256]{1,0:T(8,128)}), f32[512,256]{1,0:T(8,128)}) %all-reduce.3.cloned.1.call-update) | async-done | bytes 524304 | tf_op jit(solution)/shard_map/while/body/eval_jaxpr/psum | solution.py:53
  690.8 3.7 fusion.36
  694.5 0.0 all-reduce.5.cloned.1.call-update
  694.5 46.3 %all-reduce.5.cloned.1.call-done = f32[512,256]{0,1:T(8,128)} async-done(((f32[512,256]{0,1:T(8,128)}), f32[512,256]{0,1:T(8,128)}) %all-reduce.5.cloned.1.call-update) | async-done | bytes 524304 | tf_op jit(solution)/shard_map/while/body/eval_jaxpr/psum | solution.py:9
  740.8 1.2 copy.20
  742.0 0.8 constant_dynamic-update-slice_fusion.2
  742.9 2.3 fusion.35
  745.2 0.0 all-reduce.5.cloned.1.call-start
  745.3 149.8 %all-reduce.3.cloned.1.call-done = f32[512,256]{1,0:T(8,128)} async-done(((f32[512,256]{1,0:T(8,128)}), f32[512,256]{1,0:T(8,128)}) %all-reduce.3.cloned.1.call-update) | async-done | bytes 524304 | tf_op jit(solution)/shard_map/while/body/eval_jaxpr/psum | solution.py:53
  895.1 3.7 fusion.36
  898.8 46.3 %all-reduce.5.cloned.1.call-done = f32[512,256]{0,1:T(8,128)} async-done(((f32[512,256]{0,1:T(8,128)}), f32[512,256]{0,1:T(8,128)}) %all-reduce.5.cloned.1.call-update) | async-done | bytes 524304 | tf_op jit(solution)/shard_map/while/body/eval_jaxpr/psum | solution.py:9
  945.1 1.2 copy.20
  946.4 0.8 constant_dynamic-update-slice_fusion.2
  947.2 2.3 fusion.35
  949.5 0.0 all-reduce.3.cloned.1.call-update
  949.6 0.0 all-reduce.5.cloned.1.call-start
  949.6 149.8 %all-reduce.3.cloned.1.call-done = f32[512,256]{1,0:T(8,128)} async-done(((f32[512,256]{1,0:T(8,128)}), f32[512,256]{1,0:T(8,128)}) %all-reduce.3.cloned.1.call-update) | async-done | bytes 524304 | tf_op jit(solution)/shard_map/while/body/eval_jaxpr/psum | solution.py:53
  1099.4 3.7 fusion.36
  1103.2 46.3 %all-reduce.5.cloned.1.call-done = f32[512,256]{0,1:T(8,128)} async-done(((f32[512,256]{0,1:T(8,128)}), f32[512,256]{0,1:T(8,128)}) %all-reduce.5.cloned.1.call-update) | async-done | bytes 524304 | tf_op jit(solution)/shard_map/while/body/eval_jaxpr/psum | solution.py:9
  1149.4 1.2 copy.20
  1150.7 0.8 constant_dynamic-update-slice_fusion.2
  1151.5 1.9 constant_dynamic-slice_fusion
  (28 shorter events, 0.2 us)
Async XLA Ops:
  7.2 2.9 copy-start
  7.2 3.9 copy-start.5
  7.2 44.6 %reduce-scatter.3.cloned.1.call-start = ((), (), s32[]{:S(2)}) async-start(), calls=%async_computation.2 | async-start | bytes 2621440 | tf_op jit(solution)/shard_map/reduce_scatter | solution.py:34
  11.1 5.4 copy-start.2
  11.8 40.0 %copy-start.3 = (f32[512,512]{1,0:T(8,128)S(1)}, f32[512,512]{1,0:T(8,128)}, u32[]{:S(2)}) copy-start(f32[512,512]{1,0:T(8,128)} %param.17) | copy-start | bytes 3145732
  16.6 177.7 %reduce-scatter.5.cloned.1.call-start = ((), (), s32[]{:S(2)}) async-start(), calls=%async_computation.3 | async-start | bytes 532480 | tf_op jit(solution)/shard_map/reduce_scatter | solution.py:35
  16.6 303.9 %copy-start.4 = (f32[512,256]{1,0:T(8,128)S(1)}, f32[512,256]{1,0:T(8,128)}, u32[]{:S(2)}) copy-start(f32[512,256]{1,0:T(8,128)} %param.15) | copy-start | bytes 1572868
  52.0 270.1 %copy-start.1 = (f32[512,64]{0,1:T(8,128)S(1)}, f32[512,64]{0,1:T(8,128)}, u32[]{:S(2)}) copy-start(f32[512,64]{0,1:T(8,128)} %param.16) | copy-start | bytes 393220
  322.0 164.7 %all-reduce.3.cloned.1.call-start = ((), (), s32[]{:S(2)}) async-start(), calls=%async_computation.4 | async-start | bytes 1048576 | tf_op jit(solution)/shard_map/while/body/eval_jaxpr/psum | solution.py:53
  324.4 212.4 %all-reduce.5.cloned.1.call-start = ((), (), s32[]{:S(2)}) async-start(), calls=%async_computation.5 | async-start | bytes 1048576 | tf_op jit(solution)/shard_map/while/body/eval_jaxpr/psum | solution.py:9
  538.9 151.9 %all-reduce.3.cloned.1.call-start = ((), (), s32[]{:S(2)}) async-start(), calls=%async_computation.4 | async-start | bytes 1048576 | tf_op jit(solution)/shard_map/while/body/eval_jaxpr/psum | solution.py:53
  541.2 199.6 %all-reduce.5.cloned.1.call-start = ((), (), s32[]{:S(2)}) async-start(), calls=%async_computation.5 | async-start | bytes 1048576 | tf_op jit(solution)/shard_map/while/body/eval_jaxpr/psum | solution.py:9
  742.9 152.2 %all-reduce.3.cloned.1.call-start = ((), (), s32[]{:S(2)}) async-start(), calls=%async_computation.4 | async-start | bytes 1048576 | tf_op jit(solution)/shard_map/while/body/eval_jaxpr/psum | solution.py:53
  745.2 199.9 %all-reduce.5.cloned.1.call-start = ((), (), s32[]{:S(2)}) async-start(), calls=%async_computation.5 | async-start | bytes 1048576 | tf_op jit(solution)/shard_map/while/body/eval_jaxpr/psum | solution.py:9
  947.2 152.2 %all-reduce.3.cloned.1.call-start = ((), (), s32[]{:S(2)}) async-start(), calls=%async_computation.4 | async-start | bytes 1048576 | tf_op jit(solution)/shard_map/while/body/eval_jaxpr/psum | solution.py:53
  949.6 199.9 %all-reduce.5.cloned.1.call-start = ((), (), s32[]{:S(2)}) async-start(), calls=%async_computation.5 | async-start | bytes 1048576 | tf_op jit(solution)/shard_map/while/body/eval_jaxpr/psum | solution.py:9
Sparse Core Ops, SparseCore 0:
  16.7 35.0 reduce-scatter.2
  56.3 137.9 reduce-scatter.4
  327.2 159.4 all-reduce.2
  490.6 46.1 all-reduce.4
  543.7 146.9 all-reduce.2
  694.6 46.1 all-reduce.4
  748.1 146.9 all-reduce.2
  898.9 46.1 all-reduce.4
  952.4 146.9 all-reduce.2
  1103.3 46.1 all-reduce.4
where the time goes:
time: 1160 us
  waiting for transfers between devices  974 us (84%)
  blocking collectives  126 us (11%)
  matrix products  25.9 us (2%)
  between operations  14.2 us (1%)
  local copies, waits for them, and re-layouts  13.6 us (1%)
    psum x4, waiting for transfers between devices, step(): before = lax.psum(partial_value, 'col')  611 us
    psum x4, waiting for transfers between devices, spread(): return lax.psum(kept, axis)  185 us
    reduce_scatter x1, waiting for transfers between devices, shards(): lax.psum_scatter(row_part, ('leaf', 'col'), scatter_dimension=0, tiled=True)  142 us
    all_gather x1, blocking collectives, shards(): updates = lax.all_gather(share, ('leaf', 'col'), axis=0, tiled=True)  126 us
    reduce_scatter x1, waiting for transfers between devices, shards(): row_part = lax.psum_scatter(contrib, 'row', scatter_dimension=0, tiled=True)  35.2 us
  transfers between devices with their start and end apart: 10, of which 10 were waited for; matrix products, arithmetic and copies ran while one was open for 0% of the time, Pallas kernels for 0%

commit v1 on v0

--- a/solution.py
+++ b/solution.py
@@ -33,7 +33,10 @@
     contrib = contrib.at[targets.reshape(-1)].add(tiles.reshape(-1, right_count))
     row_part = lax.psum_scatter(contrib, "row", scatter_dimension=0, tiled=True)
     share = lax.psum_scatter(row_part, ("leaf", "col"), scatter_dimension=0, tiled=True)
-    updates = lax.all_gather(share, ("leaf", "col"), axis=0, tiled=True)
+    updates = jnp.concatenate(
+        lax.all_to_all(jnp.stack([share] * lax.axis_size(("leaf", "col"))), ("leaf", "col"), 0, 0),
+        axis=0,
+    )
     reduced = top_rhs - updates
     inverse_all = unit_lower(top_diag.reshape(owned_blocks, block_size, block_size))
     col_global = my_col * col_width + jnp.arange(col_width, dtype=jnp.int32)

time: 1160 us -> 1050 us (0.905)
  blocking collectives: 126 us -> 0 us
    all_gather x1 -> x0, blocking collectives: 126 us -> none  [shards(): updates = lax.all_gather(share, ('leaf', 'col'), axis=0, tiled=True)]
    psum x4, waiting for transfers between devices: 611 us -> 597 us  [step(): before = lax.psum(partial_value, 'col')]
    all_to_all x0 -> x1, waiting for transfers between devices: none -> 14.4 us  [shards(): lax.all_to_all(jnp.stack([share] * lax.axis_size(('leaf', 'col'))), ('lea...]
  transfers between devices with their start and end apart: 10 -> 11, of which waited for: 10 -> 11; matrix products, arithmetic and copies ran while one was open for 0% -> 0% of each run, Pallas kernels for 0% -> 0%
where the time goes in v1:
time: 1050 us; the launch traced here: 1040 us
  waiting for transfers between devices  974 us (93%)
  matrix products  25.9 us (2%)
  local copies, waits for them, and re-layouts  15.1 us (1%)
  between operations  14.2 us (1%)
    psum x4, waiting for transfers between devices, step(): before = lax.psum(partial_value, 'col')  597 us
    psum x4, waiting for transfers between devices, spread(): return lax.psum(kept, axis)  185 us
    reduce_scatter x1, waiting for transfers between devices, shards(): lax.psum_scatter(row_part, ('leaf', 'col'), scatter_dimension=0, tiled=True)  142 us
    reduce_scatter x1, waiting for transfers between devices, shards(): row_part = lax.psum_scatter(contrib, 'row', scatter_dimension=0, tiled=True)  35.2 us
  transfers between devices with their start and end apart: 11, of which 11 were waited for; matrix products, arithmetic and copies ran while one was open for 0% of the time, Pallas kernels for 0%

profile of v1, /device:TPU:8, one launch (start us, length us, event | category | flops | bytes accessed | tf_op | source)
XLA Modules:
  0.0 1045.0 jit_solution(70767380489810902)
XLA Ops:
  7.2 0.0 reduce-scatter.3.cloned.1.call-start
  7.3 0.8 iota_compare_fusion.4
  8.1 0.7 copy.23
  8.8 1.2 copy.15
  10.0 1.1 fusion.14
  11.1 0.7 convolution_select_fusion.1
  11.8 4.7 scatter_custom_fusion
  16.5 0.0 reduce-scatter.3.cloned.1.call-update
  16.6 0.0 reduce-scatter.5.cloned.1.call-start
  16.6 35.2 %reduce-scatter.3.cloned.1.call-done = f32[512,256]{1,0:T(8,128)} async-done(((f32[2048,256]{1,0:T(8,128)}), f32[512,256]{1,0:T(8,128)}) %reduce-scatter.3.cloned.1.call-update) | async-done | bytes 524304 | tf_op jit(solution)/shard_map/reduce_scatter | solution.py:34
  51.8 0.0 reduce-scatter.5.cloned.1.call-update
  51.8 142.5 %reduce-scatter.5.cloned.1.call-done = f32[8,256]{1,0:T(8,128)} async-done(((f32[512,256]{1,0:T(8,128)}), f32[8,256]{1,0:T(8,128)}) %reduce-scatter.5.cloned.1.call-update) | async-done | bytes 8208 | tf_op jit(solution)/shard_map/reduce_scatter | solution.py:35
  194.3 1.5 stack.2
  195.8 8.4 all-to-all-start
  204.2 1.4 add_bitcast_fusion
  205.6 14.4 %all-to-all-done = f32[64,8,256]{2,1,0:T(8,128)S(1)} async-done(((f32[64,8,256]{2,1,0:T(8,128)}), f32[64,8,256]{2,1,0:T(8,128)S(1)}, u32[]{:S(2)}, u32[]{:S(2)}) %all-to-all-start) | async-done | bytes 524320 | tf_op jit(solution)/shard_map/all_to_all | solution.py:37
  220.0 0.1 bitcast_subtract_fusion
  220.1 1.5 broadcast.62.clone2
  221.6 814.7 %while.16 = (s32[]{:T(128)}, f32[2048,256]{1,0:T(8,128)}, f32[512,64]{0,1:T(8,128)S(1)}, s32[]{:T(128)}, f32[512,256]{1,0:T(8,128)S(1)}, /*index=5*/f32[1,512,51...) while((s32[]{:T(128)}, f32[2048,256]{1,0:T(8,128)}, ...), condition=%wide.region_6.7_spmd.clone, body=%wide.region_3.6_spmd.clone.sunk | while | flops 906526848 | bytes 11731889 | solution.py:63
  221.6 2.3 fusion.35
  224.0 0.0 all-reduce.5.cloned.1.call-start
  224.0 147.5 %all-reduce.3.cloned.1.call-done = f32[512,256]{1,0:T(8,128)} async-done(((f32[512,256]{1,0:T(8,128)}), f32[512,256]{1,0:T(8,128)}) %all-reduce.3.cloned.1.call-update) | async-done | bytes 524304 | tf_op jit(solution)/shard_map/while/body/eval_jaxpr/psum | solution.py:56
  371.5 3.7 fusion.36
  375.2 46.3 %all-reduce.5.cloned.1.call-done = f32[512,256]{0,1:T(8,128)} async-done(((f32[512,256]{0,1:T(8,128)}), f32[512,256]{0,1:T(8,128)}) %all-reduce.5.cloned.1.call-update) | async-done | bytes 524304 | tf_op jit(solution)/shard_map/while/body/eval_jaxpr/psum | solution.py:9
  421.5 1.2 copy.25
  422.7 0.8 constant_dynamic-update-slice_fusion.2
  423.6 2.3 fusion.35
  425.9 0.0 all-reduce.5.cloned.1.call-start
  426.0 149.5 %all-reduce.3.cloned.1.call-done = f32[512,256]{1,0:T(8,128)} async-done(((f32[512,256]{1,0:T(8,128)}), f32[512,256]{1,0:T(8,128)}) %all-reduce.3.cloned.1.call-update) | async-done | bytes 524304 | tf_op jit(solution)/shard_map/while/body/eval_jaxpr/psum | solution.py:56
  575.5 3.7 fusion.36
  579.2 46.3 %all-reduce.5.cloned.1.call-done = f32[512,256]{0,1:T(8,128)} async-done(((f32[512,256]{0,1:T(8,128)}), f32[512,256]{0,1:T(8,128)}) %all-reduce.5.cloned.1.call-update) | async-done | bytes 524304 | tf_op jit(solution)/shard_map/while/body/eval_jaxpr/psum | solution.py:9
  625.5 1.2 copy.25
  626.8 0.8 constant_dynamic-update-slice_fusion.2
  627.6 2.3 fusion.35
  630.0 0.0 all-reduce.5.cloned.1.call-start
  630.0 149.8 %all-reduce.3.cloned.1.call-done = f32[512,256]{1,0:T(8,128)} async-done(((f32[512,256]{1,0:T(8,128)}), f32[512,256]{1,0:T(8,128)}) %all-reduce.3.cloned.1.call-update) | async-done | bytes 524304 | tf_op jit(solution)/shard_map/while/body/eval_jaxpr/psum | solution.py:56
  779.8 3.7 fusion.36
  783.6 46.3 %all-reduce.5.cloned.1.call-done = f32[512,256]{0,1:T(8,128)} async-done(((f32[512,256]{0,1:T(8,128)}), f32[512,256]{0,1:T(8,128)}) %all-reduce.5.cloned.1.call-update) | async-done | bytes 524304 | tf_op jit(solution)/shard_map/while/body/eval_jaxpr/psum | solution.py:9
  829.8 1.2 copy.25
  831.1 0.8 constant_dynamic-update-slice_fusion.2
  831.9 2.3 fusion.35
  834.3 0.0 all-reduce.5.cloned.1.call-start
  834.4 149.8 %all-reduce.3.cloned.1.call-done = f32[512,256]{1,0:T(8,128)} async-done(((f32[512,256]{1,0:T(8,128)}), f32[512,256]{1,0:T(8,128)}) %all-reduce.3.cloned.1.call-update) | async-done | bytes 524304 | tf_op jit(solution)/shard_map/while/body/eval_jaxpr/psum | solution.py:56
  984.1 3.7 fusion.36
  987.9 46.3 %all-reduce.5.cloned.1.call-done = f32[512,256]{0,1:T(8,128)} async-done(((f32[512,256]{0,1:T(8,128)}), f32[512,256]{0,1:T(8,128)}) %all-reduce.5.cloned.1.call-update) | async-done | bytes 524304 | tf_op jit(solution)/shard_map/while/body/eval_jaxpr/psum | solution.py:9
  1034.2 1.2 copy.25
  1035.4 0.8 constant_dynamic-update-slice_fusion.2
  1036.3 1.9 constant_dynamic-slice_fusion
  (28 shorter events, 0.2 us)
Async XLA Ops:
  7.2 2.9 copy-start
  7.2 3.9 copy-start.4
  7.2 44.6 %reduce-scatter.3.cloned.1.call-start = ((), (), s32[]{:S(2)}) async-start(), calls=%async_computation.3 | async-start | bytes 2621440 | tf_op jit(solution)/shard_map/reduce_scatter | solution.py:34
  11.1 5.4 copy-start.2
  16.6 177.7 %reduce-scatter.5.cloned.1.call-start = ((), (), s32[]{:S(2)}) async-start(), calls=%async_computation.4 | async-start | bytes 532480 | tf_op jit(solution)/shard_map/reduce_scatter | solution.py:35
  51.8 168.2 %copy-start.3 = (f32[512,256]{1,0:T(8,128)S(1)}, f32[512,256]{1,0:T(8,128)}, u32[]{:S(2)}) copy-start(f32[512,256]{1,0:T(8,128)} %param.15) | copy-start | bytes 1572868
  195.8 24.2 %all-to-all-start = ((f32[64,8,256]{2,1,0:T(8,128)}), f32[64,8,256]{2,1,0:T(8,128)S(1)}, u32[]{:S(2)}, u32[]{:S(2)}) async-start(f32[64,8,256]{2,1,0:T(8,128)} %stack.2), calls=%async_computation.2 | async-start | bytes 1048576 | tf_op jit(solution)/shard_map/all_to_all | solution.py:37
  205.6 16.0 %copy-start.1 = (f32[512,64]{0,1:T(8,128)S(1)}, f32[512,64]{0,1:T(8,128)}, u32[]{:S(2)}) copy-start(f32[512,64]{0,1:T(8,128)} %param.16) | copy-start | bytes 393220
  221.6 149.9 %all-reduce.3.cloned.1.call-start = ((), (), s32[]{:S(2)}) async-start(), calls=%async_computation.5 | async-start | bytes 1048576 | tf_op jit(solution)/shard_map/while/body/eval_jaxpr/psum | solution.py:56
  224.0 197.5 %all-reduce.5.cloned.1.call-start = ((), (), s32[]{:S(2)}) async-start(), calls=%async_computation.6 | async-start | bytes 1048576 | tf_op jit(solution)/shard_map/while/body/eval_jaxpr/psum | solution.py:9
  423.6 151.9 %all-reduce.3.cloned.1.call-start = ((), (), s32[]{:S(2)}) async-start(), calls=%async_computation.5 | async-start | bytes 1048576 | tf_op jit(solution)/shard_map/while/body/eval_jaxpr/psum | solution.py:56
  425.9 199.6 %all-reduce.5.cloned.1.call-start = ((), (), s32[]{:S(2)}) async-start(), calls=%async_computation.6 | async-start | bytes 1048576 | tf_op jit(solution)/shard_map/while/body/eval_jaxpr/psum | solution.py:9
  627.6 152.2 %all-reduce.3.cloned.1.call-start = ((), (), s32[]{:S(2)}) async-start(), calls=%async_computation.5 | async-start | bytes 1048576 | tf_op jit(solution)/shard_map/while/body/eval_jaxpr/psum | solution.py:56
  630.0 199.9 %all-reduce.5.cloned.1.call-start = ((), (), s32[]{:S(2)}) async-start(), calls=%async_computation.6 | async-start | bytes 1048576 | tf_op jit(solution)/shard_map/while/body/eval_jaxpr/psum | solution.py:9
  831.9 152.2 %all-reduce.3.cloned.1.call-start = ((), (), s32[]{:S(2)}) async-start(), calls=%async_computation.5 | async-start | bytes 1048576 | tf_op jit(solution)/shard_map/while/body/eval_jaxpr/psum | solution.py:56
  834.3 199.9 %all-reduce.5.cloned.1.call-start = ((), (), s32[]{:S(2)}) async-start(), calls=%async_computation.6 | async-start | bytes 1048576 | tf_op jit(solution)/shard_map/while/body/eval_jaxpr/psum | solution.py:9
Sparse Core Ops, SparseCore 0:
  16.7 35.0 reduce-scatter.2
  56.3 137.9 reduce-scatter.4
  226.8 144.6 all-reduce.2
  375.3 46.1 all-reduce.4
  428.5 146.9 all-reduce.2
  579.3 46.1 all-reduce.4
  632.8 146.9 all-reduce.2
  783.7 46.1 all-reduce.4
  837.1 146.9 all-reduce.2
  988.0 46.1 all-reduce.4
